TPU v7x, 128 devices: a whole 4x4x4 slice. The times are simulated.
128 devices in a mesh: fsdp: 16 (over x, z), dp: 8 (over y, core).
Axes of the slice: x: 4, y: 4, z: 4, core: 2. Of those that a mesh axis runs over, the one named last changes fastest.
Arguments:
- grad_parts: bfloat16 [8, 16384, 2048], P('dp', 'fsdp'), may hold values from -6 to 6
- old_master: float32 [16384, 2048], P(('fsdp', 'dp')), may hold values from -0.25 to 0.25
- old_mean: bfloat16 [16384, 2048], P(('fsdp', 'dp')), may hold values from -1 to 1
- old_mean_scale: bfloat16 [16384], P(('fsdp', 'dp')), may hold values from 0.049804688 to 0.5
- old_square: bfloat16 [16384, 2048], P(('fsdp', 'dp')), may hold values from 0.049804688 to 1
- old_square_scale: bfloat16 [16384], P(('fsdp', 'dp')), may hold values from 0.29882812 to 3
- old_map: int32 [16384], replicated, may hold values from 0 to 16383, as said below
Outputs:
- weights: bfloat16 [16384, 2048], P('fsdp')
- master: float32 [16384, 2048], P(('fsdp', 'dp'))
- mean_codes: bfloat16 [16384, 2048], P(('fsdp', 'dp'))
- mean_scales: bfloat16 [16384], P(('fsdp', 'dp'))
- square_codes: bfloat16 [16384, 2048], P(('fsdp', 'dp'))
- square_scales: bfloat16 [16384], P(('fsdp', 'dp'))
Inputs may be any that keep to these rules, and one draw needn't show every extreme that they name: old_map is a permutation of the old slots; old slot s lies on device s // 128 counted along fsdp+dp with fsdp major, and block b belongs to new owner b // 128 counted the same way. Every device holds exactly 128 old slots; one device holds at most 2 blocks of one new owner, and every draw has a pair with exactly 2.
All inputs are finite; a program needn't handle non-finite values. Where the computation divides by a largest or mean magnitude, that divisor is 1e-20 or more.
Results may differ from a plain program's by a relative error of at most 0.02.
Values may be sent and summed in bfloat16 or wider, within the bound.
No kernel may reach another device: no remote copies, remote signals or barrier semaphores. Data moves between devices by JAX's collectives and lax.ppermute only.
A program may use at most 64 MiB of HBM per device.

v0:
```python
import jax
import jax.numpy as jnp
from jax import lax
from jax.sharding import PartitionSpec as P


def pair_rank(owners, keyed):
    matching = owners[:, None] == owners[None, :]
    before = keyed[None, :] < keyed[:, None]
    return jnp.sum(jnp.where(matching & before, 1, 0), axis=1).astype(jnp.int32)


def route_bf16(chooser, values):
    flat_values = values.reshape((values.shape[0], -1))
    moved = jnp.dot(chooser.astype(jnp.bfloat16), flat_values, preferred_element_type=jnp.float32)
    return moved.astype(jnp.bfloat16).reshape((chooser.shape[0],) + values.shape[1:])


def route_f32(chooser, values):
    return jnp.dot(
        chooser.astype(jnp.float32),
        values,
        precision=lax.Precision.HIGHEST,
        preferred_element_type=jnp.float32,
    )


def block_peak(values):
    return (jnp.max(values, axis=1) + 1e-06).astype(jnp.bfloat16)


def local(grad_parts, old_master, old_mean, old_mean_scale, old_square, old_square_scale, old_map):
    count_all = lax.axis_size(("fsdp", "dp"))
    block_rows = old_master.shape[0]
    block_len = old_master.shape[1]
    peer_cap = max(2, 2 * block_rows // count_all)
    slot_total = count_all * peer_cap
    self_index = lax.axis_index(("fsdp", "dp"))
    gradient = lax.psum_scatter(
        grad_parts[0].astype(jnp.float32).astype(jnp.bfloat16),
        "dp",
        scatter_dimension=0,
        tiled=True,
    ).astype(jnp.float32)
    total_blocks = old_map.shape[0]
    my_slots = self_index * block_rows + jnp.arange(block_rows, dtype=jnp.int32)
    block_ids = jnp.arange(total_blocks, dtype=jnp.int32)
    held_blocks = jnp.sum(
        jnp.where(old_map[None, :] == my_slots[:, None], block_ids[None, :], 0), axis=1
    )
    target = held_blocks // block_rows
    local_pos = held_blocks % block_rows
    sent_rank = pair_rank(target, local_pos)
    wanted = lax.dynamic_slice_in_dim(old_map, self_index * block_rows, block_rows)
    source = wanted // block_rows
    got_rank = pair_rank(source, jnp.arange(block_rows, dtype=jnp.int32))
    slot_ids = jnp.arange(slot_total, dtype=jnp.int32)
    send_flat = target * peer_cap + sent_rank
    placing = slot_ids[:, None] == send_flat[None, :]
    moment_codes = jnp.stack([old_mean, old_square], axis=1)
    moment_scales = jnp.stack([old_mean_scale, old_square_scale], axis=1)
    code_buffer = route_bf16(placing, moment_codes).reshape((count_all, peer_cap, 2, block_len))
    scale_buffer = route_bf16(placing, moment_scales).reshape((count_all, peer_cap, 2))
    master_buffer = route_f32(placing, old_master).reshape((count_all, peer_cap, block_len))
    code_in, scale_in = (
        lax.all_to_all(code_buffer, ("fsdp", "dp"), split_axis=0, concat_axis=0, tiled=True),
        lax.all_to_all(scale_buffer, ("fsdp", "dp"), split_axis=0, concat_axis=0, tiled=True),
    )
    master_in = lax.all_to_all(
        master_buffer.astype(jnp.bfloat16), ("fsdp", "dp"), split_axis=0, concat_axis=0, tiled=True
    ).astype(master_buffer.dtype)
    recv_flat = source * peer_cap + got_rank
    picking = recv_flat[:, None] == slot_ids[None, :]
    code_rows = route_bf16(picking, code_in.reshape((slot_total, 2, block_len))).astype(jnp.float32)
    scale_rows = route_bf16(picking, scale_in.reshape((slot_total, 2))).astype(jnp.float32)
    weight_old = route_f32(picking, master_in.reshape((slot_total, block_len)))
    mean_old = code_rows[:, 0] * scale_rows[:, 0:1]
    square_old = code_rows[:, 1] * scale_rows[:, 1:2]
    mean_next = 0.9 * mean_old + 0.1 * gradient
    square_next = 0.95 * square_old + 0.05 * gradient * gradient
    master = weight_old - 0.05 * (mean_next / (jnp.sqrt(square_next) + 1e-08) + 0.1 * weight_old)
    mean_scales = block_peak(jnp.abs(mean_next))
    square_scales = block_peak(square_next)
    mean_codes = (mean_next / mean_scales.astype(jnp.float32)[:, None]).astype(jnp.bfloat16)
    square_codes = (square_next / square_scales.astype(jnp.float32)[:, None]).astype(jnp.bfloat16)
    weights = lax.all_gather(master.astype(jnp.bfloat16), "dp", axis=0, tiled=True)
    return (weights, master, mean_codes, mean_scales, square_codes, square_scales)


def solution(mesh):
    in_specs = (
        P("dp", "fsdp", None),
        P(("fsdp", "dp"), None),
        P(("fsdp", "dp"), None),
        P(("fsdp", "dp")),
        P(("fsdp", "dp"), None),
        P(("fsdp", "dp")),
        P(),
    )
    out_specs = (
        P("fsdp", None),
        P(("fsdp", "dp"), None),
        P(("fsdp", "dp"), None),
        P(("fsdp", "dp")),
        P(("fsdp", "dp"), None),
        P(("fsdp", "dp")),
    )
    return jax.shard_map(local, mesh=mesh, in_specs=in_specs, out_specs=out_specs, check_vma=False)
```

profile of v0, /device:TPU:1, one launch (start us, length us, event | category | flops | bytes accessed | tf_op | source)
XLA Modules:
  0.0 145.3 jit_solution(600305273660461602)
XLA Ops:
  7.3 0.7 reduce-scatter.2.cloned.1.call-update
  7.9 0.2 copy-done.4
  8.1 1.3 select_reduce_fusion
  9.5 0.2 select_reduce_fusion.1
  10.0 0.7 copy.29
  10.7 11.5 %all-to-all-start.2 = ((bf16[128,2,2]{1,2,0:T(2,128)(2,1)}), bf16[128,2,2]{1,2,0:T(2,128)(2,1)S(1)}, u32[]{:S(2)}, u32[]{:S(2)}) async-start(bf16[128,2,2]{1,2,0:T(2,128)(2,1)} %copy.29), calls=%async_computation.2 | async-start | bytes 131072 | tf_op jit(solution)/shard_map/all_to_all | solution.py:67
  22.2 1.0 convolution_convert_fusion.2
  23.3 1.5 %convert_element_type.77 = bf16[128,2,2048]{2,1,0:T(2,128)(2,1)} reshape(bf16[256,2048]{1,0:T(8,128)(2,1)S(1)} %convolution_convert_fusion.2) | data formatting | bytes 2097152 | tf_op jit(solution)/shard_map/convert_element_type | solution.py:70
  24.8 6.9 %all-to-all-done.2 = bf16[128,2,2]{1,2,0:T(2,128)(2,1)S(1)} async-done(((bf16[128,2,2]{1,2,0:T(2,128)(2,1)}), bf16[128,2,2]{1,2,0:T(2,128)(2,1)S(1)}, u32[]{:S(2)}, u32[]{:S(2)}) %all-to-all-start.2) | async-done | bytes 1056 | tf_op jit(solution)/shard_map/all_to_all | solution.py:67
  31.7 5.4 %all-to-all-start = ((bf16[128,2,2048]{2,1,0:T(2,128)(2,1)}), bf16[128,2,2048]{2,1,0:T(2,128)(2,1)}, u32[]{:S(2)}, u32[]{:S(2)}) async-start(bf16[128,2,2048]{2,1,0:T(2,128)(2,1)} %convert_element_type.77), calls=%async_computation | async-start | bytes 2097152 | tf_op jit(solution)/shard_map/all_to_all | solution.py:69
  37.0 0.3 copy.25
  37.3 0.3 copy.26
  37.7 0.7 convolution_convert_fusion
  38.4 2.8 %reshape_reshape.6 = bf16[128,2,2,2048]{3,2,1,0:T(2,128)(2,1)} reshape(bf16[256,4096]{1,0:T(8,128)(2,1)S(1)} %convolution_convert_fusion) | data formatting | bytes 4194304 | tf_op jit(solution)/shard_map/reshape;reshape | solution.py:62
  41.2 14.7 %all-to-all-done = bf16[128,2,2048]{2,1,0:T(2,128)(2,1)} async-done(((bf16[128,2,2048]{2,1,0:T(2,128)(2,1)}), bf16[128,2,2048]{2,1,0:T(2,128)(2,1)}, u32[]{:S(2)}, u32[]{:S(2)}) %all-to-all-start) | async-done | bytes 1048608 | tf_op jit(solution)/shard_map/all_to_all | solution.py:69
  55.9 5.8 %all-to-all-start.1 = ((bf16[128,2,2,2048]{3,2,1,0:T(2,128)(2,1)}), bf16[128,2,2,2048]{3,2,1,0:T(2,128)(2,1)S(1)}, u32[]{:S(2)}, u32[]{:S(2)}) async-start(bf16[128,2,2,2048]{3,2,1,0:T(2,128)(2,1)} %reshape_reshape.6), calls=%async_computation.1 | async-start | bytes 4194304 | tf_op jit(solution)/shard_map/all_to_all | solution.py:66
  61.7 0.2 all-gather.2.cloned.1.call-start
  62.4 0.2 fusion.1
  62.6 2.3 %reshape.113 = bf16[256,2048]{1,0:T(8,128)(2,1)} reshape(bf16[128,2,2048]{2,1,0:T(2,128)(2,1)} %all-to-all-done) | data formatting | bytes 2097152 | tf_op jit(solution)/shard_map/reshape | solution.py:76
  64.9 27.1 %all-to-all-done.1 = bf16[128,2,2,2048]{3,2,1,0:T(2,128)(2,1)S(1)} async-done(((bf16[128,2,2,2048]{3,2,1,0:T(2,128)(2,1)}), bf16[128,2,2,2048]{3,2,1,0:T(2,128)(2,1)S(1)}, u32[]{:S(2)}, u32[]{:S(2)}) %all-to-all-start.1) | async-done | bytes 2097184 | tf_op jit(solution)/shard_map/all_to_all | solution.py:66
  92.1 0.9 copy.34
  93.0 1.8 %fusion = f32[128,4096]{1,0:T(8,128)} fusion(bf16[256,4096]{1,0:T(8,128)(2,1)S(1)} %bitcast.49, s32[128]{0:T(128)S(1)} %multiply_add_fusion.1), kind=kOutput, calls=%fused_computation.3 | convolution fusion | flops 269516800 | bytes 4194816 | tf_op jit(solution)/shard_map/dot_general | solution.py:15
  94.8 1.9 %copy.27 = f32[128,4096]{0,1:T(8,128)S(1)} copy(f32[128,4096]{1,0:T(8,128)} %fusion) | data formatting | bytes 4194304 | tf_op jit(solution)/shard_map/convert_element_type | solution.py:74
  96.7 1.5 fusion.21
  98.1 1.6 %copy.33 = f32[128,1,2048]{2,0,1:T(8,128)S(1)} copy(f32[128,1,2048]{0,2,1:T(8,128)} %get-tuple-element.12) | data formatting | bytes 2097152
  99.7 1.6 %copy.32 = f32[128,1,2048]{2,0,1:T(8,128)S(1)} copy(f32[128,1,2048]{0,2,1:T(8,128)} %get-tuple-element.13) | data formatting | bytes 2097152
  101.3 3.5 %fusion.22 = (bf16[128,2048]{1,0:T(8,128)(2,1)}, f32[128,2048]{1,0:T(8,128)}) fusion(f32[128]{0:T(128)S(1)} %get-tuple-element.16, f32[128,1,2048]{2,0,1:T(8,128)S(1)} %copy.33, bf16[128,2048]{1,0:T(8,128)(2,1)} %reduce-scatter.2.cloned.1.call-done, f32[128]{0:T(128)S(1)} %get-tuple-element.17, f32[128,1,2048]{2,0,1:T(8,128)S(1)} %copy.32, ...), kind=kOutput, calls=%fused_computation.58 | convolution fusion | flops 138706944 | bytes 5244416 | tf_op jit(solution)/shard_map/dot_general | solution.py:20
  104.9 1.7 %fusion.18 = (f32[128]{0:T(128)S(1)}, f32[128]{0:T(128)S(1)}) fusion(bf16[128,2048]{1,0:T(8,128)(2,1)} %reduce-scatter.2.cloned.1.call-done, f32[128]{0:T(128)S(1)} %get-tuple-element.16, f32[128,1,2048]{2,0,1:T(8,128)S(1)} %copy.33, f32[128]{0:T(128)S(1)} %get-tuple-element.17, f32[128,1,2048]{2,0,1:T(8,128)S(1)} %copy.32), kind=kLoop, calls=%fused_computation.54 | loop fusion | flops 3407616 | bytes 2623488 | tf_op jit(solution)/shard_map/reduce_max | solution.py:29
  106.5 0.5 fusion.19
  107.1 1.4 divide_convert_fusion
  108.5 25.1 %all-gather.2.cloned.1.call-done = bf16[1024,2048]{1,0:T(8,128)(2,1)} async-done(((bf16[128,2048]{1,0:T(8,128)(2,1)}), bf16[1024,2048]{1,0:T(8,128)(2,1)}) %all-gather.2.cloned.1.call-update) | async-done | bytes 4194320 | tf_op jit(solution)/shard_map/all_gather | solution.py:86
  133.6 4.8 %copy.36 = bf16[1024,2048]{1,0:T(8,128)(2,1)} copy(bf16[1024,2048]{1,0:T(8,128)(2,1)} %all-gather.2.cloned.1.call-done) | data formatting | bytes 8388608
  (28 shorter events, 1.1 us)
Async XLA Ops:
  7.2 15.1 %copy-start = (f32[128,2048]{1,0:T(8,128)S(1)}, f32[128,2048]{1,0:T(8,128)}, u32[]{:S(2)}) copy-start(f32[128,2048]{1,0:T(8,128)} %param.8) | copy-start | bytes 3145732
  7.2 94.1 %reduce-scatter.2.cloned.1.call-start = ((), (), s32[]{:S(2)}) async-start(), calls=%async_computation.4 | async-start | bytes 4718592 | tf_op jit(solution)/shard_map/reduce_scatter | solution.py:39
  7.2 0.9 copy-start.4
  7.2 2.4 %copy-start.5 = (bf16[128]{0:T(256)(128)(2,1)S(1)}, bf16[128]{0:T(256)(128)(2,1)}, u32[]{:S(2)}) copy-start(bf16[128]{0:T(256)(128)(2,1)} %param.12) | copy-start | bytes 772
  7.2 2.4 %copy-start.6 = (bf16[128]{0:T(256)(128)(2,1)S(1)}, bf16[128]{0:T(256)(128)(2,1)}, u32[]{:S(2)}) copy-start(bf16[128]{0:T(256)(128)(2,1)} %param.10) | copy-start | bytes 772
  10.7 20.9 %all-to-all-start.2 = ((bf16[128,2,2]{1,2,0:T(2,128)(2,1)}), bf16[128,2,2]{1,2,0:T(2,128)(2,1)S(1)}, u32[]{:S(2)}, u32[]{:S(2)}) async-start(bf16[128,2,2]{1,2,0:T(2,128)(2,1)} %copy.29), calls=%async_computation.2 | async-start | bytes 131072 | tf_op jit(solution)/shard_map/all_to_all | solution.py:67
  23.3 13.8 %copy-start.2 = (bf16[128,2048]{1,0:T(8,128)(2,1)S(1)}, bf16[128,2048]{1,0:T(8,128)(2,1)}, u32[]{:S(2)}) copy-start(bf16[128,2048]{1,0:T(8,128)(2,1)} %param.9) | copy-start | bytes 1572868
  23.3 14.0 %copy-start.3 = (bf16[128,2048]{1,0:T(8,128)(2,1)S(1)}, bf16[128,2048]{1,0:T(8,128)(2,1)}, u32[]{:S(2)}) copy-start(bf16[128,2048]{1,0:T(8,128)(2,1)} %param.11) | copy-start | bytes 1572868
  31.7 24.2 %all-to-all-start = ((bf16[128,2,2048]{2,1,0:T(2,128)(2,1)}), bf16[128,2,2048]{2,1,0:T(2,128)(2,1)}, u32[]{:S(2)}, u32[]{:S(2)}) async-start(bf16[128,2,2048]{2,1,0:T(2,128)(2,1)} %convert_element_type.77), calls=%async_computation | async-start | bytes 2097152 | tf_op jit(solution)/shard_map/all_to_all | solution.py:69
  55.9 36.2 %all-to-all-start.1 = ((bf16[128,2,2,2048]{3,2,1,0:T(2,128)(2,1)}), bf16[128,2,2,2048]{3,2,1,0:T(2,128)(2,1)S(1)}, u32[]{:S(2)}, u32[]{:S(2)}) async-start(bf16[128,2,2,2048]{3,2,1,0:T(2,128)(2,1)} %reshape_reshape.6), calls=%async_computation.1 | async-start | bytes 4194304 | tf_op jit(solution)/shard_map/all_to_all | solution.py:66
  61.7 72.0 %all-gather.2.cloned.1.call-start = ((), (), s32[]{:S(2)}) async-start(), calls=%async_computation.5 | async-start | bytes 4718592 | tf_op jit(solution)/shard_map/all_gather | solution.py:86
  104.9 2.2 %copy-start.1 = (bf16[128,2048]{1,0:T(8,128)(2,1)S(1)}, bf16[128,2048]{1,0:T(8,128)(2,1)}, u32[]{:S(2)}) copy-start(bf16[128,2048]{1,0:T(8,128)(2,1)} %reduce-scatter.2.cloned.1.call-done) | copy-start | bytes 1572868
Sparse Core Ops, SparseCore 0:
  10.4 50.0 reduce-scatter.1
  105.0 28.6 all-gather.1
where the time goes:
time: 146 us; the launch traced here: 145 us
  waiting for transfers between devices  74.5 us (51%)
  starting transfers between devices  22.9 us (16%)
  local copies, waits for them, and re-layouts  20.5 us (14%)
  between operations  14.3 us (10%)
  matrix products  7.42 us (5%)
  other arithmetic  5.6 us (4%)
    all_to_all x1, waiting for transfers between devices, local(): lax.all_to_all(code_buffer, ('fsdp', 'dp'), split_axis=0, concat_axis=0,...  27.1 us
    all_gather x1, waiting for transfers between devices, local(): lax.all_gather(master.astype(jnp.bfloat16), 'dp', axis=0, tiled=True)  25.1 us
    all_to_all x1, waiting for transfers between devices, local(): lax.all_to_all(master_buffer.astype(jnp.bfloat16), ('fsdp', 'dp'), split_...  14.7 us
    all_to_all x1, starting transfers between devices, local(): lax.all_to_all(scale_buffer, ('fsdp', 'dp'), split_axis=0, concat_axis=0,...  11.5 us
    unnamed x20, local copies, waits for them, and re-layouts  9.58 us
    all_to_all x1, waiting for transfers between devices, local(): lax.all_to_all(scale_buffer, ('fsdp', 'dp'), split_axis=0, concat_axis=0,...  6.87 us
    all_to_all x1, starting transfers between devices, local(): lax.all_to_all(code_buffer, ('fsdp', 'dp'), split_axis=0, concat_axis=0,...  5.78 us
    all_to_all x1, starting transfers between devices, local(): lax.all_to_all(master_buffer.astype(jnp.bfloat16), ('fsdp', 'dp'), split_...  5.36 us
  transfers between devices with their start and end apart: 5, of which 4 were waited for; matrix products, arithmetic and copies ran while one was open for 17% of the time, Pallas kernels for 0%

commit v1 on v0

--- a/solution.py
+++ b/solution.py
@@ -83,7 +83,10 @@
     square_scales = block_peak(square_next)
     mean_codes = (mean_next / mean_scales.astype(jnp.float32)[:, None]).astype(jnp.bfloat16)
     square_codes = (square_next / square_scales.astype(jnp.float32)[:, None]).astype(jnp.bfloat16)
-    weights = lax.all_gather(master.astype(jnp.bfloat16), "dp", axis=0, tiled=True)
+    weights = jnp.concatenate(
+        lax.all_to_all(jnp.stack([master.astype(jnp.bfloat16)] * lax.axis_size("dp")), "dp", 0, 0),
+        axis=0,
+    )
     return (weights, master, mean_codes, mean_scales, square_codes, square_scales)
 
 

time: 146 us -> 174 us (1.19)
  waiting for transfers between devices: 74.5 us -> 94.9 us
  starting transfers between devices: 22.9 us -> 28.2 us
  local copies, waits for them, and re-layouts: 20.5 us -> 23.1 us
    all_to_all x0 -> x1, waiting for transfers between devices: none -> 45.3 us  [local(): lax.all_to_all(jnp.stack([master.astype(jnp.bfloat16)] * lax.axis_size('d...]
    all_gather x1 -> x0, waiting for transfers between devices: 25.1 us -> none  [local(): lax.all_gather(master.astype(jnp.bfloat16), 'dp', axis=0, tiled=True)]
    all_to_all x0 -> x1, starting transfers between devices: none -> 5.53 us  [local(): lax.all_to_all(jnp.stack([master.astype(jnp.bfloat16)] * lax.axis_size('d...]
    another operation x0 -> x1, local copies, waits for them, and re-layouts: none -> 2.54 us  [local(): jnp.stack([master.astype(jnp.bfloat16)] * lax.axis_size('dp'))]
  transfers between devices with their start and end apart: 5 -> 5, of which waited for: 4 -> 4; matrix products, arithmetic and copies ran while one was open for 17% -> 14% of each run, Pallas kernels for 0% -> 0%
where the time goes in v1:
time: 174 us; the launch traced here: 173 us
  waiting for transfers between devices  94.9 us (55%)
  starting transfers between devices  28.2 us (16%)
  local copies, waits for them, and re-layouts  23.1 us (13%)
  between operations  14.3 us (8%)
  matrix products  7.25 us (4%)
  other arithmetic  5.6 us (3%)
    all_to_all x1, waiting for transfers between devices, local(): lax.all_to_all(jnp.stack([master.astype(jnp.bfloat16)] * lax.axis_size('d...  45.3 us
    all_to_all x1, waiting for transfers between devices, local(): lax.all_to_all(code_buffer, ('fsdp', 'dp'), split_axis=0, concat_axis=0,...  27.4 us
    all_to_all x1, waiting for transfers between devices, local(): lax.all_to_all(master_buffer.astype(jnp.bfloat16), ('fsdp', 'dp'), split_...  14.7 us
    all_to_all x1, starting transfers between devices, local(): lax.all_to_all(scale_buffer, ('fsdp', 'dp'), split_axis=0, concat_axis=0,...  11.5 us
    unnamed x20, local copies, waits for them, and re-layouts  9.58 us
    all_to_all x1, waiting for transfers between devices, local(): lax.all_to_all(scale_buffer, ('fsdp', 'dp'), split_axis=0, concat_axis=0,...  6.87 us
    all_to_all x1, starting transfers between devices, local(): lax.all_to_all(code_buffer, ('fsdp', 'dp'), split_axis=0, concat_axis=0,...  5.78 us
    all_to_all x1, starting transfers between devices, local(): lax.all_to_all(jnp.stack([master.astype(jnp.bfloat16)] * lax.axis_size('d...  5.53 us
  transfers between devices with their start and end apart: 5, of which 4 were waited for; matrix products, arithmetic and copies ran while one was open for 14% of the time, Pallas kernels for 0%

profile of v1, /device:TPU:1, one launch (start us, length us, event | category | flops | bytes accessed | tf_op | source)
XLA Modules:
  0.0 173.3 jit_solution(10838769354415888807)
XLA Ops:
  7.3 0.7 reduce-scatter.2.cloned.1.call-update
  7.9 0.2 copy-done.4
  8.1 1.3 select_reduce_fusion
  10.0 0.7 copy.29
  10.7 11.5 %all-to-all-start.2 = ((bf16[128,2,2]{1,2,0:T(2,128)(2,1)}), bf16[128,2,2]{1,2,0:T(2,128)(2,1)S(1)}, u32[]{:S(2)}, u32[]{:S(2)}) async-start(bf16[128,2,2]{1,2,0:T(2,128)(2,1)} %copy.29), calls=%async_computation.2 | async-start | bytes 131072 | tf_op jit(solution)/shard_map/all_to_all | solution.py:67
  22.2 1.0 convolution_convert_fusion.2
  23.3 1.5 convert_element_type.77
  24.8 6.9 %all-to-all-done.2 = bf16[128,2,2]{1,2,0:T(2,128)(2,1)S(1)} async-done(((bf16[128,2,2]{1,2,0:T(2,128)(2,1)}), bf16[128,2,2]{1,2,0:T(2,128)(2,1)S(1)}, u32[]{:S(2)}, u32[]{:S(2)}) %all-to-all-start.2) | async-done | bytes 1056 | tf_op jit(solution)/shard_map/all_to_all | solution.py:67
  31.7 5.4 %all-to-all-start = ((bf16[128,2,2048]{2,1,0:T(2,128)(2,1)}), bf16[128,2,2048]{2,1,0:T(2,128)(2,1)}, u32[]{:S(2)}, u32[]{:S(2)}) async-start(bf16[128,2,2048]{2,1,0:T(2,128)(2,1)} %convert_element_type.77), calls=%async_computation | async-start | bytes 2097152 | tf_op jit(solution)/shard_map/all_to_all | solution.py:69
  37.0 0.3 copy.25
  37.3 0.3 copy.26
  37.7 0.7 convolution_convert_fusion
  38.4 2.8 %reshape_reshape.6 = bf16[128,2,2,2048]{3,2,1,0:T(2,128)(2,1)} reshape(bf16[256,4096]{1,0:T(8,128)(2,1)S(1)} %convolution_convert_fusion) | data formatting | bytes 4194304 | tf_op jit(solution)/shard_map/reshape;reshape | solution.py:62
  41.2 14.7 %all-to-all-done = bf16[128,2,2048]{2,1,0:T(2,128)(2,1)} async-done(((bf16[128,2,2048]{2,1,0:T(2,128)(2,1)}), bf16[128,2,2048]{2,1,0:T(2,128)(2,1)}, u32[]{:S(2)}, u32[]{:S(2)}) %all-to-all-start) | async-done | bytes 1048608 | tf_op jit(solution)/shard_map/all_to_all | solution.py:69
  55.9 5.8 %all-to-all-start.1 = ((bf16[128,2,2,2048]{3,2,1,0:T(2,128)(2,1)}), bf16[128,2,2,2048]{3,2,1,0:T(2,128)(2,1)S(1)}, u32[]{:S(2)}, u32[]{:S(2)}) async-start(bf16[128,2,2,2048]{3,2,1,0:T(2,128)(2,1)} %reshape_reshape.6), calls=%async_computation.1 | async-start | bytes 4194304 | tf_op jit(solution)/shard_map/all_to_all | solution.py:66
  62.2 0.2 fusion.1
  62.4 2.3 %reshape.118 = bf16[256,2048]{1,0:T(8,128)(2,1)} reshape(bf16[128,2,2048]{2,1,0:T(2,128)(2,1)} %all-to-all-done) | data formatting | bytes 2097152 | tf_op jit(solution)/shard_map/reshape | solution.py:76
  64.7 27.4 %all-to-all-done.1 = bf16[128,2,2,2048]{3,2,1,0:T(2,128)(2,1)S(1)} async-done(((bf16[128,2,2,2048]{3,2,1,0:T(2,128)(2,1)}), bf16[128,2,2,2048]{3,2,1,0:T(2,128)(2,1)S(1)}, u32[]{:S(2)}, u32[]{:S(2)}) %all-to-all-start.1) | async-done | bytes 2097184 | tf_op jit(solution)/shard_map/all_to_all | solution.py:66
  92.1 0.9 copy.34
  93.0 1.8 %fusion = f32[128,4096]{1,0:T(8,128)} fusion(bf16[256,4096]{1,0:T(8,128)(2,1)S(1)} %bitcast.50, s32[128]{0:T(128)S(1)} %multiply_add_fusion.1), kind=kOutput, calls=%fused_computation.3 | convolution fusion | flops 269516800 | bytes 4194816 | tf_op jit(solution)/shard_map/dot_general | solution.py:15
  94.8 1.9 %copy.27 = f32[128,4096]{0,1:T(8,128)S(1)} copy(f32[128,4096]{1,0:T(8,128)} %fusion) | data formatting | bytes 4194304 | tf_op jit(solution)/shard_map/convert_element_type | solution.py:74
  96.7 1.5 fusion.21
  98.1 1.6 copy.33
  99.7 1.6 copy.32
  101.3 3.4 %fusion.22 = (bf16[128,2048]{1,0:T(8,128)(2,1)S(1)}, f32[128,2048]{1,0:T(8,128)}) fusion(f32[128]{0:T(128)S(1)} %get-tuple-element.16, f32[128,1,2048]{2,0,1:T(8,128)S(1)} %copy.33, bf16[128,2048]{1,0:T(8,128)(2,1)} %reduce-scatter.2.cloned.1.call-done, f32[128]{0:T(128)S(1)} %get-tuple-element.17, f32[128,1,2048]{2,0,1:T(8,128)S(1)} %copy.32, ...), kind=kOutput, calls=%fused_computation.58 | convolution fusion | flops 138706944 | bytes 5244416 | tf_op jit(solution)/shard_map/dot_general | solution.py:20
  104.7 2.5 %stack.35 = bf16[8,128,2048]{2,1,0:T(8,128)(2,1)} broadcast(bf16[128,2048]{1,0:T(8,128)(2,1)S(1)} %get-tuple-element.20), dimensions={1,2} | broadcast | bytes 4718592 | tf_op jit(solution)/shard_map/stack | solution.py:87
  107.2 5.5 %all-to-all-start.3 = ((bf16[8,128,2048]{2,1,0:T(8,128)(2,1)}), bf16[8,128,2048]{2,1,0:T(8,128)(2,1)}, u32[]{:S(2)}, u32[]{:S(2)}) async-start(bf16[8,128,2048]{2,1,0:T(8,128)(2,1)} %stack.35), calls=%async_computation.4 | async-start | bytes 8388608 | tf_op jit(solution)/shard_map/all_to_all | solution.py:87
  112.7 1.7 fusion.18
  114.4 0.5 fusion.19
  114.9 1.4 divide_convert_fusion
  116.4 45.3 %all-to-all-done.3 = bf16[8,128,2048]{2,1,0:T(8,128)(2,1)} async-done(((bf16[8,128,2048]{2,1,0:T(8,128)(2,1)}), bf16[8,128,2048]{2,1,0:T(8,128)(2,1)}, u32[]{:S(2)}, u32[]{:S(2)}) %all-to-all-start.3) | async-done | bytes 4194336 | tf_op jit(solution)/shard_map/all_to_all | solution.py:87
  161.7 4.8 %copy.36 = bf16[1024,2048]{1,0:T(8,128)(2,1)} copy(bf16[1024,2048]{1,0:T(8,128)(2,1)} %bitcast.11) | data formatting | bytes 8388608
  (28 shorter events, 1.2 us)
Async XLA Ops:
  7.2 15.1 %copy-start = (f32[128,2048]{1,0:T(8,128)S(1)}, f32[128,2048]{1,0:T(8,128)}, u32[]{:S(2)}) copy-start(f32[128,2048]{1,0:T(8,128)} %param.8) | copy-start | bytes 3145732
  7.2 94.1 %reduce-scatter.2.cloned.1.call-start = ((), (), s32[]{:S(2)}) async-start(), calls=%async_computation.5 | async-start | bytes 4718592 | tf_op jit(solution)/shard_map/reduce_scatter | solution.py:39
  7.2 0.9 copy-start.4
  7.2 2.4 %copy-start.5 = (bf16[128]{0:T(256)(128)(2,1)S(1)}, bf16[128]{0:T(256)(128)(2,1)}, u32[]{:S(2)}) copy-start(bf16[128]{0:T(256)(128)(2,1)} %param.12) | copy-start | bytes 772
  7.2 2.4 %copy-start.6 = (bf16[128]{0:T(256)(128)(2,1)S(1)}, bf16[128]{0:T(256)(128)(2,1)}, u32[]{:S(2)}) copy-start(bf16[128]{0:T(256)(128)(2,1)} %param.10) | copy-start | bytes 772
  10.7 20.9 %all-to-all-start.2 = ((bf16[128,2,2]{1,2,0:T(2,128)(2,1)}), bf16[128,2,2]{1,2,0:T(2,128)(2,1)S(1)}, u32[]{:S(2)}, u32[]{:S(2)}) async-start(bf16[128,2,2]{1,2,0:T(2,128)(2,1)} %copy.29), calls=%async_computation.2 | async-start | bytes 131072 | tf_op jit(solution)/shard_map/all_to_all | solution.py:67
  23.3 13.8 %copy-start.2 = (bf16[128,2048]{1,0:T(8,128)(2,1)S(1)}, bf16[128,2048]{1,0:T(8,128)(2,1)}, u32[]{:S(2)}) copy-start(bf16[128,2048]{1,0:T(8,128)(2,1)} %param.9) | copy-start | bytes 1572868
  23.3 14.0 %copy-start.3 = (bf16[128,2048]{1,0:T(8,128)(2,1)S(1)}, bf16[128,2048]{1,0:T(8,128)(2,1)}, u32[]{:S(2)}) copy-start(bf16[128,2048]{1,0:T(8,128)(2,1)} %param.11) | copy-start | bytes 1572868
  31.7 24.2 %all-to-all-start = ((bf16[128,2,2048]{2,1,0:T(2,128)(2,1)}), bf16[128,2,2048]{2,1,0:T(2,128)(2,1)}, u32[]{:S(2)}, u32[]{:S(2)}) async-start(bf16[128,2,2048]{2,1,0:T(2,128)(2,1)} %convert_element_type.77), calls=%async_computation | async-start | bytes 2097152 | tf_op jit(solution)/shard_map/all_to_all | solution.py:69
  55.9 36.2 %all-to-all-start.1 = ((bf16[128,2,2,2048]{3,2,1,0:T(2,128)(2,1)}), bf16[128,2,2,2048]{3,2,1,0:T(2,128)(2,1)S(1)}, u32[]{:S(2)}, u32[]{:S(2)}) async-start(bf16[128,2,2,2048]{3,2,1,0:T(2,128)(2,1)} %reshape_reshape.6), calls=%async_computation.1 | async-start | bytes 4194304 | tf_op jit(solution)/shard_map/all_to_all | solution.py:66
  107.2 54.5 %all-to-all-start.3 = ((bf16[8,128,2048]{2,1,0:T(8,128)(2,1)}), bf16[8,128,2048]{2,1,0:T(8,128)(2,1)}, u32[]{:S(2)}, u32[]{:S(2)}) async-start(bf16[8,128,2048]{2,1,0:T(8,128)(2,1)} %stack.35), calls=%async_computation.4 | async-start | bytes 8388608 | tf_op jit(solution)/shard_map/all_to_all | solution.py:87
  112.7 2.2 %copy-start.1 = (bf16[128,2048]{1,0:T(8,128)(2,1)S(1)}, bf16[128,2048]{1,0:T(8,128)(2,1)}, u32[]{:S(2)}) copy-start(bf16[128,2048]{1,0:T(8,128)(2,1)} %reduce-scatter.2.cloned.1.call-done) | copy-start | bytes 1572868
Sparse Core Ops, SparseCore 0:
  10.4 50.0 reduce-scatter.1
